TPU v7x, 128 devices: a whole 4x4x4 slice. The times are simulated.
128 devices in a mesh: feat: 8 (over x_lo, y), dp: 16 (over z, x_hi, core).
Axes of the slice: x: 4 (x_hi: 2, x_lo: 2; x = x_hi * 2 + x_lo), y: 4, z: 4, core: 2. Of those that a mesh axis runs over, the one named last changes fastest.
Arguments:
- text_rows: bfloat16 [2048, 8192], P('dp', 'feat'), may hold values from -6 to 6
- q_weight: bfloat16 [8192, 8192], P(None, 'feat'), may hold values from -0.0625 to 0.0625
- features: bfloat16 [16, 1024, 7680], P('dp', None, 'feat'), may hold values from -6 to 6
- kv_weight: bfloat16 [7680, 2048], P('feat'), may hold values from -0.0625 to 0.0625
- q_gain: float32 [128], replicated, may hold values from 0.7 to 2.6
- k_gain: float32 [128], replicated, may hold values from 0.7 to 2.6
- attn_gate: float32 [1], replicated, may hold values from 0.5 to 2
- image_ids: int32 [256, 2], P('dp'), may hold values from 0 to 15, all different within a row; in each aligned block of 16 rows (0 to 15, 16 to 31, ...) at most 4 rows name the same one
- image_slot: int32 [16], replicated, may hold values from 0 to 15, each once
Outputs:
- attended: bfloat16 [2048, 8192], P('dp', 'feat')
Inputs may be any that keep to these rules, and one draw needn't show every extreme that they name: `image_ids`: each request names two different images; among the requests of one index of dp (aligned blocks of 16 requests) no image is named more than 4 times, a bound that some block reaches. Each position once; image i lies at position image_slot[i].
All inputs are finite; a program needn't handle non-finite values.
Results may differ from a plain program's by a relative error of at most 0.009.
The roundings to bfloat16 on the way count: a program that leaves them out, or rounds other values in their place, can miss the bound.
Values may be sent and summed in bfloat16 or wider, within the bound.
No kernel may reach another device: no remote copies, remote signals or barrier semaphores. Data moves between devices by JAX's collectives and lax.ppermute only.
A program may use at most 128 MiB of HBM per device.

v0:
```python
import jax
import jax.numpy as jnp
from jax import lax
from jax.sharding import PartitionSpec as P

epsilon = 1e-05


def head_norm(values, gain_vector):
    return (
        values
        * lax.rsqrt(jnp.mean(values * values, axis=-1, keepdims=True) + epsilon)
        * gain_vector
    )


def attend(queries, keyval, weights):
    head_width = queries.shape[-1]
    scores = jnp.einsum(
        "rhgd,hnd->rhgn", queries, keyval[..., :head_width], preferred_element_type=jnp.float32
    )
    exponent = jnp.exp(scores)
    exponent = exponent * weights[:, None, None, None]
    exponent = exponent.astype(jnp.bfloat16)
    denominator = jnp.sum(exponent.astype(jnp.float32), axis=-1)
    numerator = jnp.einsum(
        "rhgn,hnd->rhgd", exponent, keyval[..., head_width:], preferred_element_type=jnp.float32
    )
    return (numerator, denominator)


def per_device(
    text_rows, q_weight, features, kv_weight, q_gain, k_gain, attn_gate, image_ids, image_slot
):
    row_count = text_rows.shape[0]
    requests = image_ids.shape[0]
    text_words = row_count // requests
    head_width = q_gain.shape[0]
    heads_all = kv_weight.shape[1] // (2 * head_width)
    kv_local = heads_all // lax.axis_size("feat")
    group_size = q_weight.shape[1] // (head_width * kv_local)
    weight_block = q_weight
    queries = jnp.dot(
        lax.all_gather(text_rows, "feat", axis=1, tiled=True),
        weight_block,
        preferred_element_type=jnp.float32,
    )
    queries = head_norm(
        queries.reshape(row_count, kv_local, group_size, head_width), q_gain
    ) * head_width ** (-0.5)
    queries = queries.astype(jnp.bfloat16)
    kv_table = kv_weight.reshape(kv_weight.shape[0], heads_all, 2 * head_width)
    vision_rows = features[0]
    weight_block = kv_table
    summed = lax.psum_scatter(
        jnp.einsum("nf,fhc->hnc", vision_rows, weight_block, preferred_element_type=jnp.float32),
        "feat",
        scatter_dimension=0,
        tiled=True,
    )
    normed_keys = head_norm(summed[..., :head_width], k_gain)
    keyval = jnp.concatenate([normed_keys, summed[..., head_width:]], axis=-1).astype(jnp.bfloat16)
    image_count = image_slot.shape[0]
    matches = image_ids[:, :, None] == jnp.arange(image_count, dtype=jnp.int32)[None, None, :]
    owners = jnp.sum(jnp.where(matches, image_slot[None, None, :], 0), axis=-1)
    starting = (
        jnp.zeros((row_count, kv_local, group_size, head_width), jnp.float32),
        jnp.zeros((row_count, kv_local, group_size), jnp.float32),
    )
    shard_piece = lax.all_gather(keyval[None], "dp", axis=0, tiled=True)

    def add_one(position, partial_sums):
        reads_image = jnp.any(owners == position, axis=1)
        weights = jnp.repeat(reads_image.astype(jnp.float32), text_words)
        kv_block = lax.dynamic_index_in_dim(shard_piece, position, 0, keepdims=False)
        numerator, denominator = attend(queries, kv_block, weights)
        return (partial_sums[0] + numerator, partial_sums[1] + denominator)

    numerator, denominator = lax.fori_loop(0, shard_piece.shape[0], add_one, starting)
    result = numerator / denominator[..., None]
    return (jnp.tanh(attn_gate[0]) * result).astype(jnp.bfloat16).reshape(row_count, -1)


def solution(mesh):
    in_specs = (
        P("dp", "feat"),
        P(None, "feat"),
        P("dp", None, "feat"),
        P("feat", None),
        P(),
        P(),
        P(),
        P("dp", None),
        P(),
    )
    out_specs = P("dp", "feat")
    return jax.shard_map(
        per_device, mesh=mesh, in_specs=in_specs, out_specs=out_specs, check_vma=False
    )
```

profile of v0, /device:TPU:1, one launch (start us, length us, event | category | flops | bytes accessed | tf_op | source)
XLA Modules:
  0.0 329.7 jit_solution(1036196203318548550)
XLA Ops:
  8.1 9.0 %fusion.13 = f32[8,1024,256]{1,2,0:T(8,128)} fusion(bf16[120,8,8,256]{3,2,1,0:T(8,128)(2,1)} %bitcast.86, bf16[1,1024,960]{1,2,0:T(8,128)(2,1)S(1)} %copy-done), kind=kOutput, calls=%fused_computation.16 | convolution fusion | flops 4026531840 | bytes 14286848 | tf_op jit(solution)/shard_map/nf,fhc->hnc/dot_general | solution.py:56
  17.9 95.3 %reduce-scatter.2.cloned.1.call-done = f32[1,1024,256]{1,2,0:T(8,128)} async-done(((f32[8,1024,256]{1,2,0:T(8,128)}), f32[1,1024,256]{1,2,0:T(8,128)}) %reduce-scatter.2.cloned.1.call-update) | async-done | bytes 1048592 | tf_op jit(solution)/shard_map/reduce_scatter | solution.py:55
  118.5 31.4 %all-gather.5.cloned.1.call-done = bf16[128,8192]{1,0:T(8,128)(2,1)} async-done(((bf16[128,1024]{1,0:T(8,128)(2,1)}), bf16[128,8192]{1,0:T(8,128)(2,1)}) %all-gather.5.cloned.1.call-update) | async-done | bytes 2097168 | tf_op jit(solution)/shard_map/all_gather | solution.py:44
  149.9 8.7 %convolution_bitcast_fusion = f32[16,8,8,128]{3,1,2,0:T(8,128)S(1)} fusion(bf16[128,8192]{1,0:T(8,128)(2,1)} %all-gather.5.cloned.1.call-done, bf16[8192,1024]{1,0:T(8,128)(2,1)} %param.12), kind=kOutput, calls=%fused_computation.18 | convolution fusion | flops 2147483648 | bytes 19398656 | tf_op jit(solution)/shard_map/dot_general | solution.py:43
  159.3 71.2 %all-gather.3.cloned.1.call-done = bf16[16,1,1024,256]{3,2,1,0:T(8,128)(2,1)} async-done(((bf16[1,1,1024,256]{3,2,1,0:T(8,128)(2,1)}), bf16[16,1,1024,256]{3,2,1,0:T(8,128)(2,1)}) %all-gather.3.cloned.1.call-update) | async-done | bytes 8388624 | tf_op jit(solution)/shard_map/all_gather | solution.py:70
  230.5 91.7 %while.16 = (s32[]{:T(128)}, f32[128,1,8,128]{0,3,2,1:T(8,128)S(1)}, f32[128,1,8]{0,2,1:T(8,128)S(1)}, bf16[16,1,1024,256]{3,2,1,0:T(8,128)(2,1)}, bf16[128,1,8,...) while((s32[]{:T(128)}, f32[128,1,8,128]{0,3,2,1:T(8,128)S(1)}, ...), condition=%wide.region_7.8_spmd.clone, body=%wide.region_4.7_spmd.clone.sunk | while | flops 541328448 | bytes 7096712 | solution.py:79
  231.8 2.3 convert_reduce_fusion.2
  234.1 2.1 fusion.27
  237.5 2.3 convert_reduce_fusion.2
  239.8 2.1 fusion.27
  243.2 2.3 convert_reduce_fusion.2
  249.0 2.3 convert_reduce_fusion.2
  254.7 2.3 convert_reduce_fusion.2
  260.4 2.3 convert_reduce_fusion.2
  266.2 2.3 convert_reduce_fusion.2
  271.9 2.3 convert_reduce_fusion.2
  277.6 2.3 convert_reduce_fusion.2
  283.4 2.3 convert_reduce_fusion.2
  289.1 2.3 convert_reduce_fusion.2
  294.9 2.3 convert_reduce_fusion.2
  300.6 2.3 convert_reduce_fusion.2
  306.3 2.3 convert_reduce_fusion.2
  312.1 2.3 convert_reduce_fusion.2
  317.8 2.3 convert_reduce_fusion.2
  (142 shorter events, 58.8 us)
Async XLA Ops:
  6.5 1.5 copy-start
  6.5 106.6 %reduce-scatter.2.cloned.1.call-start = ((), (), s32[]{:S(2)}) async-start(), calls=%async_computation.1 | async-start | bytes 9437184 | tf_op jit(solution)/shard_map/reduce_scatter | solution.py:55
  17.1 98.3 %copy-start.3 = (f32[128]{0:T(128)S(1)}, f32[128]{0:T(128)}, u32[]{:S(2)}) copy-start(f32[128]{0:T(128)} %param.16) | copy-start | bytes 1540
  17.1 101.2 %copy-start.1 = (s32[16,2]{0,1:T(2,128)S(1)}, s32[16,2]{0,1:T(2,128)}, u32[]{:S(2)}) copy-start(s32[16,2]{0,1:T(2,128)} %param.18) | copy-start | bytes 388
  17.1 101.2 %copy-start.2 = (s32[16]{0:T(128)S(1)}, s32[16]{0:T(128)}, u32[]{:S(2)}) copy-start(s32[16]{0:T(128)} %param.19) | copy-start | bytes 196
  17.1 132.8 %all-gather.5.cloned.1.call-start = ((), (), s32[]{:S(2)}) async-start(), calls=%async_computation.3 | async-start | bytes 2359296 | tf_op jit(solution)/shard_map/all_gather | solution.py:44
  17.9 212.6 %all-gather.3.cloned.1.call-start = ((), (), s32[]{:S(2)}) async-start(), calls=%async_computation.2 | async-start | bytes 8912896 | tf_op jit(solution)/shard_map/all_gather | solution.py:70
  118.5 40.5 %copy-start.4 = (f32[128]{0:T(128)S(1)}, f32[128]{0:T(128)}, u32[]{:S(2)}) copy-start(f32[128]{0:T(128)} %param.15) | copy-start | bytes 1540
Sparse Core Ops, SparseCore 0:
  17.2 95.9 reduce-scatter.1
  114.8 35.0 all-gather.4
  152.4 78.0 all-gather.2
where the time goes:
time: 331 us; the launch traced here: 330 us
  waiting for transfers between devices  199 us (60%)
  matrix products  88.4 us (27%)
  local copies, waits for them, and re-layouts  24.5 us (7%)
  between operations  13.9 us (4%)
  other arithmetic  3.55 us (1%)
    reduce_scatter x1, waiting for transfers between devices, per_device(): lax.psum_scatter(jnp.einsum('nf,fhc->hnc', vision_rows, weight_block, pre...  95.3 us
    all_gather x1, waiting for transfers between devices, per_device(): shard_piece = lax.all_gather(keyval[None], 'dp', axis=0, tiled=True)  71.2 us
    dot_general x16, matrix products, attend(): jnp.einsum('rhgd,hnd->rhgn', queries, keyval[..., :head_width], preferred...  36.6 us
    dot_general x16, matrix products, attend(): jnp.einsum('rhgn,hnd->rhgd', exponent, keyval[..., head_width:], preferre...  34.2 us
    all_gather x1, waiting for transfers between devices, per_device(): lax.all_gather(text_rows, 'feat', axis=1, tiled=True)  31.4 us
    squeeze x16, local copies, waits for them, and re-layouts, add_one(): lax.dynamic_index_in_dim(shard_piece, position, 0, keepdims=False)  17.3 us
    dot_general x1, matrix products, per_device(): jnp.einsum('nf,fhc->hnc', vision_rows, weight_block, preferred_element_ty...  8.98 us
    dot_general x1, matrix products, per_device(): jnp.dot(lax.all_gather(text_rows, 'feat', axis=1, tiled=True), weight_blo...  8.74 us
  transfers between devices with their start and end apart: 3, of which 3 were waited for; matrix products, arithmetic and copies ran while one was open for 4% of the time, Pallas kernels for 0%

commit v1 on v0

--- a/solution.py
+++ b/solution.py
@@ -67,7 +67,13 @@
         jnp.zeros((row_count, kv_local, group_size, head_width), jnp.float32),
         jnp.zeros((row_count, kv_local, group_size), jnp.float32),
     )
-    shard_piece = lax.all_gather(keyval[None], "dp", axis=0, tiled=True)
+    matrix = keyval[None]
+    shard_piece = jnp.concatenate(
+        lax.all_to_all(
+            jnp.stack(lax.psum(1, "dp") * [matrix], axis=0), "dp", split_axis=0, concat_axis=0
+        ),
+        axis=0,
+    )
 
     def add_one(position, partial_sums):
         reads_image = jnp.any(owners == position, axis=1)

time: 331 us -> 345 us (1.042)
  starting transfers between devices: 0.08 us -> 7.37 us
    all_gather x1 -> x0, waiting for transfers between devices: 71.2 us -> none  [per_device(): shard_piece = lax.all_gather(keyval[None], 'dp', axis=0, tiled=True)]
    all_to_all x0 -> x1, waiting for transfers between devices: none -> 52.3 us  [per_device(): lax.all_to_all(jnp.stack(lax.psum(1, 'dp') * [matrix], axis=0), 'dp', spl...]
    all_gather x1, waiting for transfers between devices: 31.4 us -> 52.6 us  [per_device(): lax.all_gather(text_rows, 'feat', axis=1, tiled=True)]
    all_to_all x0 -> x1, starting transfers between devices: none -> 7.33 us  [per_device(): lax.all_to_all(jnp.stack(lax.psum(1, 'dp') * [matrix], axis=0), 'dp', spl...]
    another operation x0 -> x1, local copies, waits for them, and re-layouts: none -> 4.02 us  [per_device(): jnp.stack(lax.psum(1, 'dp') * [matrix], axis=0)]
  transfers between devices with their start and end apart: 3 -> 3, of which waited for: 3 -> 3; matrix products, arithmetic and copies ran while one was open for 4% -> 3% of each run, Pallas kernels for 0% -> 0%
where the time goes in v1:
time: 345 us; the launch traced here: 344 us
  waiting for transfers between devices  202 us (59%)
  matrix products  88.4 us (26%)
  local copies, waits for them, and re-layouts  27.7 us (8%)
  between operations  14.2 us (4%)
  starting transfers between devices  7.37 us (2%)
  other arithmetic  3.55 us (1%)
    reduce_scatter x1, waiting for transfers between devices, per_device(): lax.psum_scatter(jnp.einsum('nf,fhc->hnc', vision_rows, weight_block, pre...  96.1 us
    all_gather x1, waiting for transfers between devices, per_device(): lax.all_gather(text_rows, 'feat', axis=1, tiled=True)  52.6 us
    all_to_all x1, waiting for transfers between devices, per_device(): lax.all_to_all(jnp.stack(lax.psum(1, 'dp') * [matrix], axis=0), 'dp', spl...  52.3 us
    dot_general x16, matrix products, attend(): jnp.einsum('rhgd,hnd->rhgn', queries, keyval[..., :head_width], preferred...  36.6 us
    dot_general x16, matrix products, attend(): jnp.einsum('rhgn,hnd->rhgd', exponent, keyval[..., head_width:], preferre...  34.2 us
    squeeze x16, local copies, waits for them, and re-layouts, add_one(): lax.dynamic_index_in_dim(shard_piece, position, 0, keepdims=False)  17.3 us
    dot_general x1, matrix products, per_device(): jnp.einsum('nf,fhc->hnc', vision_rows, weight_block, preferred_element_ty...  8.98 us
    dot_general x1, matrix products, per_device(): jnp.dot(lax.all_gather(text_rows, 'feat', axis=1, tiled=True), weight_blo...  8.74 us
  transfers between devices with their start and end apart: 3, of which 3 were waited for; matrix products, arithmetic and copies ran while one was open for 3% of the time, Pallas kernels for 0%

profile of v1, /device:TPU:1, one launch (start us, length us, event | category | flops | bytes accessed | tf_op | source)
XLA Modules:
  0.0 343.6 jit_solution(243336457351436233)
XLA Ops:
  8.1 9.0 %fusion.13 = f32[8,1024,256]{1,2,0:T(8,128)} fusion(bf16[120,8,8,256]{3,2,1,0:T(8,128)(2,1)} %bitcast.89, bf16[1,1024,960]{1,2,0:T(8,128)(2,1)S(1)} %copy-done), kind=kOutput, calls=%fused_computation.16 | convolution fusion | flops 4026531840 | bytes 14286848 | tf_op jit(solution)/shard_map/nf,fhc->hnc/dot_general | solution.py:56
  17.1 96.1 %reduce-scatter.2.cloned.1.call-done = f32[1,1024,256]{1,2,0:T(8,128)} async-done(((f32[8,1024,256]{1,2,0:T(8,128)}), f32[1,1024,256]{1,2,0:T(8,128)}) %reduce-scatter.2.cloned.1.call-update) | async-done | bytes 1048592 | tf_op jit(solution)/shard_map/reduce_scatter | solution.py:55
  116.8 4.0 %stack.3 = bf16[16,1,1,1024,256]{4,3,2,1,0:T(8,128)(2,1)} broadcast(bf16[1024,256]{1,0:T(8,128)(2,1)S(1)} %copy.44), dimensions={3,4} | broadcast | bytes 8912896 | tf_op jit(solution)/shard_map/stack | solution.py:73
  120.8 7.3 %all-to-all-start = ((bf16[16,1,1,1024,256]{4,3,2,1,0:T(8,128)(2,1)}), bf16[16,1,1,1024,256]{4,3,2,1,0:T(8,128)(2,1)}, u32[]{:S(2)}, u32[]{:S(2)}) async-start(bf16[16,1,1,1024,256]{4,3,2,1,0:T(8,128)(2,1)} %stack.3), calls=%async_computation.1 | async-start | bytes 16777216 | tf_op jit(solution)/shard_map/all_to_all | solution.py:72
  129.8 52.6 %all-gather.2.cloned.1.call-done = bf16[128,8192]{1,0:T(8,128)(2,1)} async-done(((bf16[128,1024]{1,0:T(8,128)(2,1)}), bf16[128,8192]{1,0:T(8,128)(2,1)}) %all-gather.2.cloned.1.call-update) | async-done | bytes 2097168 | tf_op jit(solution)/shard_map/all_gather | solution.py:44
  182.4 8.7 %convolution_bitcast_fusion = f32[16,8,8,128]{3,1,2,0:T(8,128)S(1)} fusion(bf16[128,8192]{1,0:T(8,128)(2,1)} %all-gather.2.cloned.1.call-done, bf16[8192,1024]{1,0:T(8,128)(2,1)} %param.12), kind=kOutput, calls=%fused_computation.18 | convolution fusion | flops 2147483648 | bytes 19398656 | tf_op jit(solution)/shard_map/dot_general | solution.py:43
  191.7 52.3 %all-to-all-done = bf16[16,1,1,1024,256]{4,3,2,1,0:T(8,128)(2,1)} async-done(((bf16[16,1,1,1024,256]{4,3,2,1,0:T(8,128)(2,1)}), bf16[16,1,1,1024,256]{4,3,2,1,0:T(8,128)(2,1)}, u32[]{:S(2)}, u32[]{:S(2)}) %all-to-all-start) | async-done | bytes 8388640 | tf_op jit(solution)/shard_map/all_to_all | solution.py:72
  244.1 91.7 %while.16 = (s32[]{:T(128)}, f32[128,1,8,128]{0,3,2,1:T(8,128)S(1)}, f32[128,1,8]{0,2,1:T(8,128)S(1)}, bf16[16,1,1024,256]{3,2,1,0:T(8,128)(2,1)}, bf16[128,1,8,...) while((s32[]{:T(128)}, f32[128,1,8,128]{0,3,2,1:T(8,128)S(1)}, ...), condition=%wide.region_7.8_spmd.clone, body=%wide.region_4.7_spmd.clone.sunk | while | flops 541328448 | bytes 7096712 | solution.py:85
  245.4 2.3 convert_reduce_fusion.2
  251.1 2.3 convert_reduce_fusion.2
  256.8 2.3 convert_reduce_fusion.2
  262.6 2.3 convert_reduce_fusion.2
  268.3 2.3 convert_reduce_fusion.2
  274.0 2.3 convert_reduce_fusion.2
  279.8 2.3 convert_reduce_fusion.2
  285.5 2.3 convert_reduce_fusion.2
  291.2 2.3 convert_reduce_fusion.2
  297.0 2.3 convert_reduce_fusion.2
  302.7 2.3 convert_reduce_fusion.2
  308.4 2.3 convert_reduce_fusion.2
  314.2 2.3 convert_reduce_fusion.2
  319.9 2.3 convert_reduce_fusion.2
  325.6 2.3 convert_reduce_fusion.2
  331.4 2.3 convert_reduce_fusion.2
  (142 shorter events, 62.1 us)
Async XLA Ops:
  6.5 1.5 copy-start
  6.5 106.6 %reduce-scatter.2.cloned.1.call-start = ((), (), s32[]{:S(2)}) async-start(), calls=%async_computation.2 | async-start | bytes 9437184 | tf_op jit(solution)/shard_map/reduce_scatter | solution.py:55
  17.1 98.3 %copy-start.3 = (f32[128]{0:T(128)S(1)}, f32[128]{0:T(128)}, u32[]{:S(2)}) copy-start(f32[128]{0:T(128)} %param.16) | copy-start | bytes 1540
  120.8 8.8 %copy-start.1 = (s32[16,2]{0,1:T(2,128)S(1)}, s32[16,2]{0,1:T(2,128)}, u32[]{:S(2)}) copy-start(s32[16,2]{0,1:T(2,128)} %param.18) | copy-start | bytes 388
  120.8 8.8 %copy-start.2 = (s32[16]{0:T(128)S(1)}, s32[16]{0:T(128)}, u32[]{:S(2)}) copy-start(s32[16]{0:T(128)} %param.19) | copy-start | bytes 196
  120.8 123.3 %all-to-all-start = ((bf16[16,1,1,1024,256]{4,3,2,1,0:T(8,128)(2,1)}), bf16[16,1,1,1024,256]{4,3,2,1,0:T(8,128)(2,1)}, u32[]{:S(2)}, u32[]{:S(2)}) async-start(bf16[16,1,1,1024,256]{4,3,2,1,0:T(8,128)(2,1)} %stack.3), calls=%async_computation.1 | async-start | bytes 16777216 | tf_op jit(solution)/shard_map/all_to_all | solution.py:72
  128.1 54.2 %all-gather.2.cloned.1.call-start = ((), (), s32[]{:S(2)}) async-start(), calls=%async_computation.3 | async-start | bytes 2359296 | tf_op jit(solution)/shard_map/all_gather | solution.py:44
  129.8 61.7 %copy-start.4 = (f32[128]{0:T(128)S(1)}, f32[128]{0:T(128)}, u32[]{:S(2)}) copy-start(f32[128]{0:T(128)} %param.15) | copy-start | bytes 1540
Sparse Core Ops, SparseCore 0:
  17.2 95.9 reduce-scatter.1
  130.6 51.7 all-gather.1
